TPU v7x, 512 devices: a whole 4x4x16 slice. The times are simulated.
512 devices in a mesh: row: 32 (over z, core), col: 16 (over x, y).
Axes of the slice: x: 4, y: 4, z: 16, core: 2. Of those that a mesh axis runs over, the one named last changes fastest.
Arguments:
- front_entries: float32 [16384, 16384], P('row', 'col'), may hold values from 0 to 3, as said below
- tile_group: int32 [32], replicated, may hold values from 0 to 3
- child_factor: bfloat16 [16384, 256], P('row', 'col'), may hold values from -0.375 to 0.375
- row_map: int32 [128], replicated, may hold values from 0 to 127, as said below
Outputs:
- factor_panels: bfloat16 [16384, 512], P('row', 'col')
- schur_block: float32 [16384, 16384], P('row', 'col')
Inputs may be any that keep to these rules, and one draw needn't show every extreme that they name: `front_entries`: Symmetric; assembled is positive definite. `row_map`: A permutation of the parent tiles. The tile in row block r (blocks of 512 rows) goes to a parent tile in row block r or in the row block whose index differs from r in the highest bit.
All inputs are finite; a program needn't handle non-finite values.
Results may differ from a plain program's by a relative error of at most 0.0026.
Values may be sent and summed in bfloat16 or wider, within the bound.
A program may use at most 64 MiB of HBM per device.

v0:
```python
import jax
import jax.numpy as jnp
from jax import lax
from jax.sharding import PartitionSpec as P

PW = 256
NP = 2
TS = 128
MT = 512


def swapped(value, axis, stride):
    mask = 2**stride
    pairs = [(source, source ^ mask) for source in range(lax.axis_size(axis))]
    return lax.ppermute(value, axis, pairs)


def broadcast(value, axis, source):
    kept = jnp.where(lax.axis_index(axis) == source, value, 0).astype(value.dtype)
    return lax.psum(kept, axis)


def panel_columns(matrix, offset, width_cols, fan_ratio, block_rows):
    return jnp.concatenate(
        [
            matrix[:, q * block_rows + offset : q * block_rows + offset + width_cols]
            for q in range(fan_ratio)
        ],
        axis=1,
    )


def outer_rows(left, right):
    return jnp.einsum("ik,jk->ij", left, right, preferred_element_type=jnp.float32)


def subtract_block(matrix, lead_rows, owner, low, col_from, col_to, base_col):
    region = matrix[low:, base_col + col_from : base_col + col_to]
    return matrix.at[low:, base_col + col_from : base_col + col_to].set(
        region - outer_rows(lead_rows, owner[col_from:col_to])
    )


def right_solve(lower_factor, strip):
    return lax.linalg.triangular_solve(
        lower_factor, strip, left_side=False, lower=True, transpose_a=True
    )


def local(front_entries, tile_group, child_factor, row_map):
    row_count = lax.axis_size("row")
    col_count = lax.axis_size("col")
    fan_ratio = row_count // col_count
    local_rows = front_entries.shape[0]
    local_cols = front_entries.shape[1]
    my_row = lax.axis_index("row")
    my_col = lax.axis_index("col")
    row_tiles = local_rows // MT
    col_tiles = local_cols // MT
    group_rows = lax.dynamic_slice_in_dim(tile_group, my_row * row_tiles, row_tiles)
    group_cols = lax.dynamic_slice_in_dim(tile_group, my_col * col_tiles, col_tiles)
    same_group = (group_rows[:, None] == group_cols[None, :]).astype(jnp.float32)
    masked = (
        front_entries.reshape(row_tiles, MT, col_tiles, MT) * same_group[:, None, :, None]
    ).reshape(local_rows, local_cols)
    child_full = lax.all_gather(child_factor, "col", axis=1, tiled=True)
    child_width = child_full.shape[1]
    partner_full = swapped(child_full, "row", row_count.bit_length() - 2)
    tile_count = local_rows // TS
    partner_row = jnp.bitwise_xor(my_row, row_count // 2)
    own_map = lax.dynamic_slice_in_dim(row_map, my_row * tile_count, tile_count)
    partner_map = lax.dynamic_slice_in_dim(row_map, partner_row * tile_count, tile_count)
    slot_ids = my_row * tile_count + jnp.arange(tile_count, dtype=jnp.int32)

    def place_tiles(tile_map, source):
        chooser = (tile_map[None, :] == slot_ids[:, None]).astype(jnp.bfloat16)
        placed = jnp.dot(
            chooser,
            source.reshape(tile_count, TS * child_width),
            preferred_element_type=jnp.float32,
        )
        return placed.astype(jnp.bfloat16).reshape(local_rows, child_width)

    own_parent = place_tiles(own_map, child_full)
    partner_parent = place_tiles(partner_map, partner_full)
    lower_half = my_row < row_count // 2
    child_wide = jnp.where(
        lower_half,
        jnp.concatenate([own_parent, partner_parent], axis=1),
        jnp.concatenate([partner_parent, own_parent], axis=1),
    )
    child_owners = [broadcast(child_wide, "row", fan_ratio * my_col + q) for q in range(fan_ratio)]
    matrix = jnp.concatenate(
        [
            masked[:, q * local_rows : (q + 1) * local_rows]
            + outer_rows(child_wide, child_owners[q])
            for q in range(fan_ratio)
        ],
        axis=1,
    )
    row_share = PW // row_count
    col_share = PW // col_count
    local_ids = jnp.arange(local_rows)
    coming = None
    outputs = []
    for k in range(NP):
        offset = k * row_share
        panel_strip = panel_columns(matrix, offset, row_share, fan_ratio, local_rows)
        corner = panel_strip[offset : offset + row_share]
        gathered = lax.all_gather(corner, ("row", "col"), axis=0, tiled=True)
        diagonal = (
            gathered.reshape(row_count, col_count, row_share, col_share)
            .transpose(0, 2, 1, 3)
            .reshape(PW, PW)
        )
        lower_factor = jnp.linalg.cholesky(diagonal)
        whole_strip = lax.all_gather(panel_strip, "col", axis=1, tiled=True)
        rounded = right_solve(lower_factor, whole_strip).astype(jnp.bfloat16)
        own_lower = lax.dynamic_slice_in_dim(lower_factor, my_row * row_share, row_share).astype(
            jnp.bfloat16
        )
        rounded = jnp.where((local_ids < offset)[:, None], jnp.zeros_like(rounded), rounded)
        rounded = rounded.at[offset : offset + row_share].set(own_lower)
        outputs.append(lax.dynamic_slice_in_dim(rounded, my_col * col_share, col_share, 1))
        owners = [broadcast(rounded, "row", fan_ratio * my_col + q) for q in range(fan_ratio)]
        low = offset + row_share
        lead_rows = rounded[low:]
        for q in range(fan_ratio):
            matrix = subtract_block(
                matrix, lead_rows, owners[q], low, low, local_rows, q * local_rows
            )
    pivot_done = NP * row_share
    row_keep = local_ids >= pivot_done
    col_keep = jnp.arange(local_cols) % local_rows >= pivot_done
    schur_block = jnp.where(row_keep[:, None] & col_keep[None, :], matrix, jnp.zeros_like(matrix))
    factor_panels = jnp.concatenate(outputs, axis=1)
    return (factor_panels, schur_block)


def solution(mesh):
    placed = (P("row", "col"), P(), P("row", "col"), P())
    return jax.shard_map(
        local,
        mesh=mesh,
        in_specs=placed,
        out_specs=(P("row", "col"), P("row", "col")),
        check_vma=False,
    )
```

profile of v0, /device:TPU:1, one launch (start us, length us, event | category | flops | bytes accessed | tf_op | source)
XLA Modules:
  0.0 1302.7 jit_solution(17513636110733798873)
XLA Ops:
  7.2 19.7 %all_gather.15 = bf16[512,256]{0,1:T(8,128)(2,1)S(1)} all-gather(bf16[512,16]{0,1:T(8,128)(2,1)} %param.21), channel_id=1, replica_groups=mesh['row'=32,'col'=16] {'col'}, dimensions={1}, use_global_device_ids=true | all-gather | bytes 278528 | tf_op jit(solution)/shard_map/all_gather | solution.py:66
  26.9 15.4 %collective-permute-start = (bf16[512,256]{0,1:T(8,128)(2,1)S(1)}, bf16[512,256]{0,1:T(8,128)(2,1)S(1)}, u32[]{:S(2)}, u32[]{:S(2)}) collective-permute-start(bf16[512,256]{0,1:T(8,128)(2,1)S(1)} %all_gather.15), channel_id=1, source_target_pairs={{0,256},{16,272},{32,288},{48,304},{64,320},{80,336},{96,352},{112... | collective-permute-start | bytes 786440 | tf_op jit(solution)/shard_map/ppermute | solution.py:15
  51.2 226.5 %all-reduce.12.cloned.1.call-done = (bf16[512,512]{1,0:T(8,128)(2,1)}, bf16[512,512]{1,0:T(8,128)(2,1)}) async-done(((bf16[512,512]{1,0:T(8,128)(2,1)}, bf16[512,512]{1,0:T(8,128)(2,1)}), (bf16[512,512]{1,0:T(8,128)(2,1)}, bf16[512,512]{1,0:T(8,128)(2,1)})) %all-reduce.12.cloned.1.call-update) | async-done | bytes 1048592 | tf_op jit(solution)/shard_map/psum | solution.py:20
  281.4 198.2 %all_gather.16 = f32[4096,16]{1,0:T(8,128)S(1)} all-gather(f32[8,16]{1,0:T(8,128)S(1)} %copy.33), channel_id=1, replica_groups=mesh['row'=32,'col'=16] {'row','col'}, dimensions={0}, use_global_device_ids=true | all-gather | bytes 262656 | tf_op jit(solution)/shard_map/all_gather | solution.py:110
  481.1 11.7 cholesky.130
  492.8 9.8 custom-call.13
  503.1 11.9 cholesky.147
  517.6 3.8 while.10
  521.5 19.7 %custom-call.14 = f32[2,128,128]{1,2,0:T(8,128)S(1)} custom-call(f32[2,128,128]{2,1,0:T(8,128)S(1)} %get-tuple-element.90), custom_call_target="InvertDiagBlocksLowerTriangular" | custom-call | tf_op jit(solution)/shard_map/triangular_solve/custom-call.0 | solution.py:45
  541.2 16.2 %all_gather.17 = f32[512,256]{0,1:T(8,128)S(1)} all-gather(f32[512,16]{0,1:T(8,128)S(1)} %pad_maximum_fusion.1), channel_id=1, replica_groups=mesh['row'=32,'col'=16] {'col'}, dimensions={1}, use_global_device_ids=true | all-gather | bytes 557056 | tf_op jit(solution)/shard_map/all_gather | solution.py:117
  561.5 209.2 %all-reduce.10.cloned.1.call-done = (bf16[512,256]{0,1:T(8,128)(2,1)}, bf16[512,256]{0,1:T(8,128)(2,1)}) async-done(((bf16[512,256]{0,1:T(8,128)(2,1)}, bf16[512,256]{0,1:T(8,128)(2,1)}), (bf16[512,256]{0,1:T(8,128)(2,1)}, bf16[512,256]{0,1:T(8,128)(2,1)})) %all-reduce.10.cloned.1.call-update) | async-done | bytes 524304 | tf_op jit(solution)/shard_map/psum | solution.py:20
  773.2 5.4 scatter.21
  780.2 3.4 scatter.24
  783.8 197.6 %all_gather.18 = f32[4096,16]{1,0:T(8,128)S(1)} all-gather(f32[8,16]{1,0:T(8,128)S(1)} %copy.38), channel_id=1, replica_groups=mesh['row'=32,'col'=16] {'row','col'}, dimensions={0}, use_global_device_ids=true | all-gather | bytes 262656 | tf_op jit(solution)/shard_map/all_gather | solution.py:110
  986.0 11.7 cholesky.164
  997.8 9.8 custom-call.15
  1008.1 11.7 cholesky.181
  1022.4 4.0 while.11
  1026.5 19.9 %custom-call.16 = f32[2,128,128]{1,2,0:T(8,128)S(1)} custom-call(f32[2,128,128]{2,1,0:T(8,128)S(1)} %get-tuple-element.91), custom_call_target="InvertDiagBlocksLowerTriangular" | custom-call | tf_op jit(solution)/shard_map/triangular_solve/custom-call.0 | solution.py:45
  1046.4 16.3 %all_gather.19 = f32[512,256]{0,1:T(8,128)S(1)} all-gather(f32[512,16]{0,1:T(8,128)S(1)} %pad_maximum_fusion.2), channel_id=1, replica_groups=mesh['row'=32,'col'=16] {'col'}, dimensions={1}, use_global_device_ids=true | all-gather | bytes 557056 | tf_op jit(solution)/shard_map/all_gather | solution.py:117
  1066.2 210.0 %all-reduce.8.cloned.1.call-done = (bf16[512,256]{0,1:T(8,128)(2,1)}, bf16[512,256]{0,1:T(8,128)(2,1)}) async-done(((bf16[512,256]{0,1:T(8,128)(2,1)}, bf16[512,256]{0,1:T(8,128)(2,1)}), (bf16[512,256]{0,1:T(8,128)(2,1)}, bf16[512,256]{0,1:T(8,128)(2,1)})) %all-reduce.8.cloned.1.call-update) | async-done | bytes 524304 | tf_op jit(solution)/shard_map/psum | solution.py:20
  1278.8 5.4 scatter.26
  1285.8 5.6 scatter.29
  1293.0 2.9 copy.45
  (118 shorter events, 47.5 us)
Async XLA Ops:
  7.2 36.9 %copy-start.5 = (s32[32]{0:T(128)S(1)}, s32[32]{0:T(128)}, u32[]{:S(2)}) copy-start(s32[32]{0:T(128)} %param.20) | copy-start | bytes 388
  7.2 270.5 %all-reduce.12.cloned.1.call-start = ((), (), s32[]{:S(2)}) async-start(), calls=%async_computation.2 | async-start | bytes 2097152 | tf_op jit(solution)/shard_map/psum | solution.py:20
  26.9 20.5 %collective-permute-start = (bf16[512,256]{0,1:T(8,128)(2,1)S(1)}, bf16[512,256]{0,1:T(8,128)(2,1)S(1)}, u32[]{:S(2)}, u32[]{:S(2)}) collective-permute-start(bf16[512,256]{0,1:T(8,128)(2,1)S(1)} %all_gather.15), channel_id=1, source_target_pairs={{0,256},{16,272},{32,288},{48,304},{64,320},{80,336},{96,352},{112... | collective-permute-start | bytes 786440 | tf_op jit(solution)/shard_map/ppermute | solution.py:15
  48.3 2.9 copy-start.2
  49.6 721.1 %all-reduce.10.cloned.1.call-start = ((), (), s32[]{:S(2)}) async-start(), calls=%async_computation.1 | async-start | bytes 1048576 | tf_op jit(solution)/shard_map/psum | solution.py:20
  51.2 228.6 %copy-start = (f32[512,1024]{0,1:T(8,128)S(1)}, f32[512,1024]{0,1:T(8,128)}, u32[]{:S(2)}) copy-start(f32[512,1024]{0,1:T(8,128)} %broadcast_multiply_fusion) | copy-start | bytes 6291460
  277.7 2.1 copy-start.3
  277.7 2.1 copy-start.6
  280.3 1.0 copy-start.1
  560.0 716.2 %all-reduce.8.cloned.1.call-start = ((), (), s32[]{:S(2)}) async-start(), calls=%async_computation | async-start | bytes 1048576 | tf_op jit(solution)/shard_map/psum | solution.py:20
  1276.2 8.0 copy-start.4
Sparse Core Ops, SparseCore 0:
  49.7 227.9 all-reduce.11
  560.1 210.4 all-reduce.9
  1065.7 210.4 all-reduce.7
where the time goes:
time: 1310 us; the launch traced here: 1300 us
  waiting for transfers between devices  646 us (49%)
  blocking collectives  448 us (34%)
  other arithmetic  119 us (9%)
  local copies, waits for them, and re-layouts  42.4 us (3%)
  between operations  17.1 us (1%)
  starting transfers between devices  15.5 us (1%)
  matrix products  15 us (1%)
    psum x3, waiting for transfers between devices, broadcast(): return lax.psum(kept, axis)  646 us
    all_gather x2, blocking collectives, local(): gathered = lax.all_gather(corner, ('row', 'col'), axis=0, tiled=True)  396 us
    another operation x14, other arithmetic, local(): lower_factor = jnp.linalg.cholesky(diagonal)  69.3 us
    another operation x5, other arithmetic, right_solve(): lax.linalg.triangular_solve(lower_factor, strip, left_side=False, lower=T...  39.7 us
    all_gather x2, blocking collectives, local(): whole_strip = lax.all_gather(panel_strip, 'col', axis=1, tiled=True)  32.5 us
  transfers between devices with their start and end apart: 4, of which 3 were waited for; matrix products, arithmetic and copies ran while one was open for 1% of the time, Pallas kernels for 0%

commit v1 on v0

--- a/solution.py
+++ b/solution.py
@@ -2,6 +2,7 @@
 import jax.numpy as jnp
 from jax import lax
 from jax.sharding import PartitionSpec as P
+from jax.lax import all_to_all, psum
 
 PW = 256
 NP = 2
@@ -114,7 +115,10 @@
             .reshape(PW, PW)
         )
         lower_factor = jnp.linalg.cholesky(diagonal)
-        whole_strip = lax.all_gather(panel_strip, "col", axis=1, tiled=True)
+        carry_out = psum(1, "col")
+        long_array = jnp.stack([panel_strip] * carry_out)
+        q_next = all_to_all(long_array, "col", 0, 0)
+        whole_strip = jnp.concatenate(q_next, axis=1)
         rounded = right_solve(lower_factor, whole_strip).astype(jnp.bfloat16)
         own_lower = lax.dynamic_slice_in_dim(lower_factor, my_row * row_share, row_share).astype(
             jnp.bfloat16

time: 1310 us -> 1280 us (0.977)
  blocking collectives: 448 us -> 416 us
    all_gather x2 -> x0, blocking collectives: 32.5 us -> none  [local(): whole_strip = lax.all_gather(panel_strip, 'col', axis=1, tiled=True)]
  transfers between devices with their start and end apart: 4 -> 6, of which waited for: 3 -> 3; matrix products, arithmetic and copies ran while one was open for 1% -> 4% of each run, Pallas kernels for 0% -> 0%
where the time goes in v1:
time: 1280 us
  waiting for transfers between devices  641 us (50%)
  blocking collectives  416 us (32%)
  other arithmetic  119 us (9%)
  local copies, waits for them, and re-layouts  46.1 us (4%)
  starting transfers between devices  22.7 us (2%)
  between operations  17.2 us (1%)
  matrix products  17.1 us (1%)
    psum x3, waiting for transfers between devices, broadcast(): return lax.psum(kept, axis)  641 us
    all_gather x2, blocking collectives, local(): gathered = lax.all_gather(corner, ('row', 'col'), axis=0, tiled=True)  396 us
    another operation x14, other arithmetic, local(): lower_factor = jnp.linalg.cholesky(diagonal)  69.4 us
    another operation x5, other arithmetic, right_solve(): lax.linalg.triangular_solve(lower_factor, strip, left_side=False, lower=T...  40 us
  transfers between devices with their start and end apart: 6, of which 3 were waited for; matrix products, arithmetic and copies ran while one was open for 4% of the time, Pallas kernels for 0%

profile of v1, /device:TPU:1, one launch (start us, length us, event | category | flops | bytes accessed | tf_op | source)
XLA Modules:
  0.0 1278.8 jit_solution(12751334755396384129)
XLA Ops:
  7.2 19.7 %all_gather.9 = bf16[512,256]{0,1:T(8,128)(2,1)S(1)} all-gather(bf16[512,16]{0,1:T(8,128)(2,1)} %param.21), channel_id=1, replica_groups=mesh['row'=32,'col'=16] {'col'}, dimensions={1}, use_global_device_ids=true | all-gather | bytes 278528 | tf_op jit(solution)/shard_map/all_gather | solution.py:67
  26.9 15.4 %collective-permute-start = (bf16[512,256]{0,1:T(8,128)(2,1)S(1)}, bf16[512,256]{0,1:T(8,128)(2,1)S(1)}, u32[]{:S(2)}, u32[]{:S(2)}) collective-permute-start(bf16[512,256]{0,1:T(8,128)(2,1)S(1)} %all_gather.9), channel_id=1, source_target_pairs={{0,256},{16,272},{32,288},{48,304},{64,320},{80,336},{96,352},{112... | collective-permute-start | bytes 786440 | tf_op jit(solution)/shard_map/ppermute | solution.py:16
  51.1 226.5 %all-reduce.12.cloned.1.call-done = (bf16[512,512]{1,0:T(8,128)(2,1)}, bf16[512,512]{1,0:T(8,128)(2,1)}) async-done(((bf16[512,512]{1,0:T(8,128)(2,1)}, bf16[512,512]{1,0:T(8,128)(2,1)}), (bf16[512,512]{1,0:T(8,128)(2,1)}, bf16[512,512]{1,0:T(8,128)(2,1)})) %all-reduce.12.cloned.1.call-update) | async-done | bytes 1048592 | tf_op jit(solution)/shard_map/psum | solution.py:21
  281.3 198.2 %all_gather.10 = f32[4096,16]{1,0:T(8,128)S(1)} all-gather(f32[8,16]{1,0:T(8,128)S(1)} %copy.35), channel_id=1, replica_groups=mesh['row'=32,'col'=16] {'row','col'}, dimensions={0}, use_global_device_ids=true | all-gather | bytes 262656 | tf_op jit(solution)/shard_map/all_gather | solution.py:111
  481.0 11.7 cholesky.130
  492.8 9.8 custom-call.13
  503.1 11.9 cholesky.147
  517.2 3.6 all-to-all-start
  522.2 4.0 while.10
  526.2 19.7 %custom-call.14 = f32[2,128,128]{1,2,0:T(8,128)S(1)} custom-call(f32[2,128,128]{2,1,0:T(8,128)S(1)} %get-tuple-element.90), custom_call_target="InvertDiagBlocksLowerTriangular" | custom-call | tf_op jit(solution)/shard_map/triangular_solve/custom-call.0 | solution.py:46
  550.2 206.8 %all-reduce.10.cloned.1.call-done = (bf16[512,256]{0,1:T(8,128)(2,1)}, bf16[512,256]{0,1:T(8,128)(2,1)}) async-done(((bf16[512,256]{0,1:T(8,128)(2,1)}, bf16[512,256]{0,1:T(8,128)(2,1)}), (bf16[512,256]{0,1:T(8,128)(2,1)}, bf16[512,256]{0,1:T(8,128)(2,1)})) %all-reduce.10.cloned.1.call-update) | async-done | bytes 524304 | tf_op jit(solution)/shard_map/psum | solution.py:21
  759.6 5.4 scatter.21
  766.7 3.4 scatter.24
  770.2 197.6 %all_gather.11 = f32[4096,16]{1,0:T(8,128)S(1)} all-gather(f32[8,16]{1,0:T(8,128)S(1)} %copy.40), channel_id=1, replica_groups=mesh['row'=32,'col'=16] {'row','col'}, dimensions={0}, use_global_device_ids=true | all-gather | bytes 262656 | tf_op jit(solution)/shard_map/all_gather | solution.py:111
  972.4 11.7 cholesky.164
  984.2 9.8 custom-call.15
  994.5 11.7 cholesky.181
  1008.4 3.6 all-to-all-start.1
  1013.4 4.2 while.11
  1017.6 20.3 %custom-call.16 = f32[2,128,128]{1,2,0:T(8,128)} custom-call(f32[2,128,128]{2,1,0:T(8,128)S(1)} %get-tuple-element.91), custom_call_target="InvertDiagBlocksLowerTriangular" | custom-call | tf_op jit(solution)/shard_map/triangular_solve/custom-call.0 | solution.py:46
  1045.1 207.2 %all-reduce.8.cloned.1.call-done = (bf16[512,256]{0,1:T(8,128)(2,1)}, bf16[512,256]{0,1:T(8,128)(2,1)}) async-done(((bf16[512,256]{0,1:T(8,128)(2,1)}, bf16[512,256]{0,1:T(8,128)(2,1)}), (bf16[512,256]{0,1:T(8,128)(2,1)}, bf16[512,256]{0,1:T(8,128)(2,1)})) %all-reduce.8.cloned.1.call-update) | async-done | bytes 524304 | tf_op jit(solution)/shard_map/psum | solution.py:21
  1254.9 5.4 scatter.26
  1262.0 5.6 scatter.29
  1269.1 2.9 copy.47
  (126 shorter events, 53.3 us)
Async XLA Ops:
  7.2 36.9 %copy-start.5 = (s32[32]{0:T(128)S(1)}, s32[32]{0:T(128)}, u32[]{:S(2)}) copy-start(s32[32]{0:T(128)} %param.20) | copy-start | bytes 388
  7.2 270.5 %all-reduce.12.cloned.1.call-start = ((), (), s32[]{:S(2)}) async-start(), calls=%async_computation.4 | async-start | bytes 2097152 | tf_op jit(solution)/shard_map/psum | solution.py:21
  26.9 20.5 %collective-permute-start = (bf16[512,256]{0,1:T(8,128)(2,1)S(1)}, bf16[512,256]{0,1:T(8,128)(2,1)S(1)}, u32[]{:S(2)}, u32[]{:S(2)}) collective-permute-start(bf16[512,256]{0,1:T(8,128)(2,1)S(1)} %all_gather.9), channel_id=1, source_target_pairs={{0,256},{16,272},{32,288},{48,304},{64,320},{80,336},{96,352},{112... | collective-permute-start | bytes 786440 | tf_op jit(solution)/shard_map/ppermute | solution.py:16
  48.3 2.8 copy-start.2
  51.1 228.7 %copy-start = (f32[512,1024]{0,1:T(8,128)S(1)}, f32[512,1024]{0,1:T(8,128)}, u32[]{:S(2)}) copy-start(f32[512,1024]{0,1:T(8,128)} %broadcast_multiply_fusion) | copy-start | bytes 6291460
  277.6 2.1 copy-start.3
  277.6 2.1 copy-start.6
  280.3 1.0 copy-start.1
  517.2 28.8 %all-to-all-start = ((f32[16,512,16]{1,2,0:T(8,128)}), f32[16,512,16]{1,2,0:T(8,128)S(1)}, u32[]{:S(2)}, u32[]{:S(2)}) async-start(f32[16,512,16]{1,2,0:T(8,128)} %stack.4), calls=%async_computation | async-start | bytes 1048576 | tf_op jit(solution)/shard_map/all_to_all | solution.py:120
  520.7 236.3 %all-reduce.10.cloned.1.call-start = ((), (), s32[]{:S(2)}) async-start(), calls=%async_computation.3 | async-start | bytes 1048576 | tf_op jit(solution)/shard_map/psum | solution.py:21
  1008.4 29.6 %all-to-all-start.1 = ((f32[16,512,16]{1,2,0:T(8,128)}), f32[16,512,16]{1,2,0:T(8,128)S(1)}, u32[]{:S(2)}, u32[]{:S(2)}) async-start(f32[16,512,16]{1,2,0:T(8,128)} %stack.5), calls=%async_computation.1 | async-start | bytes 1048576 | tf_op jit(solution)/shard_map/all_to_all | solution.py:120
  1012.0 240.3 %all-reduce.8.cloned.1.call-start = ((), (), s32[]{:S(2)}) async-start(), calls=%async_computation.2 | async-start | bytes 1048576 | tf_op jit(solution)/shard_map/psum | solution.py:21
  1252.3 8.0 copy-start.4
Sparse Core Ops, SparseCore 0:
  49.7 227.9 all-reduce.11
  548.9 208.0 all-reduce.9
  1044.6 207.7 all-reduce.7
